TPU v7x, 256 devices: a whole 4x4x8 slice. The times are simulated.
256 devices in a mesh: dp: 64 (over x, z_lo, y), pipe: 4 (over z_hi, core).
Axes of the slice: x: 4, y: 4, z: 8 (z_hi: 2, z_lo: 4; z = z_hi * 4 + z_lo), core: 2. Of those that a mesh axis runs over, the one named last changes fastest.
Arguments:
- hidden: bfloat16 [16384, 2048], P('dp'), may hold values from -16 to 16
- gain: float32 [2048], replicated, may hold values from 0.25 to 1.75
- w_value: bfloat16 [4, 2048, 2048], P('pipe', 'dp'), may hold values from -0.125 to 0.125
- d_value: bfloat16 [4, 16384, 2048], P('pipe', 'dp'), may hold values from -3 to 3
Outputs:
- grad_hidden: bfloat16 [16384, 2048], P('dp')
- grad_gain: float32 [2048], P('dp')
- grad_value: float32 [4, 2048, 2048], P('pipe', 'dp')
All inputs are finite; a program needn't handle non-finite values.
Results may differ from a plain program's by a relative error of at most 0.0029.
Values may be sent and summed in bfloat16 or wider, within the bound.
No kernel may reach another device: no remote copies, remote signals or barrier semaphores. Data moves between devices by JAX's collectives and lax.ppermute only.
A program may use at most 64 MiB of HBM per device.

v0:
```python
import jax
import jax.numpy as jnp
from jax import lax
from jax.sharding import PartitionSpec as P

epsilon = 1e-06


def norm_backward(grad_rows, normed_rows, scale_rows, gain):
    scaled = gain * grad_rows
    result = (
        scaled - normed_rows * jnp.mean(scaled * normed_rows, axis=-1, keepdims=True)
    ) / scale_rows
    return (result.astype(jnp.bfloat16), jnp.sum(grad_rows * normed_rows, axis=0))


def weight_term(encoded, operand):
    return lax.dot_general(
        encoded, operand, (((0,), (0,)), ((), ())), preferred_element_type=jnp.float32
    )


def local(hidden, gain, w_value, d_value):
    hidden_f = hidden.astype(jnp.float32)
    row_scale = jnp.sqrt(jnp.mean(hidden_f * hidden_f, axis=-1, keepdims=True) + epsilon)
    normed = hidden_f / row_scale
    encoded = (normed * gain).astype(jnp.bfloat16)
    cotangent = d_value[0]
    projection = w_value[0]
    average = 1.0 / lax.axis_size("dp")
    partial_value = lax.dot_general(
        cotangent,
        lax.all_gather(projection, "dp", axis=0, tiled=True),
        (((1,), (1,)), ((), ())),
        preferred_element_type=jnp.float32,
    )
    grad_encoded = lax.psum(partial_value, "pipe")
    grad_hidden, gain_part = norm_backward(grad_encoded, normed, row_scale, gain)
    gain_share = lax.psum_scatter(gain_part, "dp", scatter_dimension=0, tiled=True)
    grad_gain = gain_share * average
    value_grad = (
        lax.psum_scatter(weight_term(encoded, cotangent), "dp", scatter_dimension=0, tiled=True)
        * average
    )
    return (grad_hidden, grad_gain, value_grad[None])


def solution(mesh):
    return jax.shard_map(
        local,
        mesh=mesh,
        in_specs=(P("dp", None), P(), P("pipe", "dp", None), P("pipe", "dp", None)),
        out_specs=(P("dp", None), P("dp"), P("pipe", "dp", None)),
        check_vma=False,
    )
```

profile of v0, /device:TPU:0, one launch (start us, length us, event | category | flops | bytes accessed | tf_op | source)
XLA Modules:
  0.0 898.9 jit_solution(13786770550400615789)
XLA Ops:
  7.2 0.0 copy-start
  7.2 0.0 all-gather.3.cloned.1.call-start
  7.2 0.7 all-gather.3.cloned.1.call-update
  7.9 0.0 all-reduce.3.cloned.1.call-start
  8.0 363.1 %all-gather.3.cloned.1.call-done = bf16[1,2048,2048]{2,1,0:T(8,128)(2,1)} async-done(((bf16[1,32,2048]{2,1,0:T(8,128)(2,1)}), bf16[1,2048,2048]{2,1,0:T(8,128)(2,1)}) %all-gather.3.cloned.1.call-update) | async-done | bytes 8388624 | tf_op jit(solution)/shard_map/all_gather | solution.py:33
  371.1 0.0 copy-done
  371.1 7.1 fusion
  378.2 0.0 copy-start.1
  378.2 0.0 copy-start.2
  378.2 0.0 all-reduce.3.cloned.1.call-update
  378.2 0.0 reduce-scatter.2.cloned.1.call-start
  378.3 1.1 copy-done.1
  379.4 0.3 fusion.2
  379.7 0.0 copy-done.2
  379.7 8.4 fusion.3
  388.1 0.0 copy-start.3
  388.1 0.0 reduce-scatter.2.cloned.1.call-update
  388.1 0.7 copy-done.3
  388.8 0.6 dynamic-slice
  390.0 87.9 %all-reduce.3.cloned.1.call-done = f32[256,2048]{1,0:T(8,128)} async-done(((f32[256,2048]{1,0:T(8,128)}), f32[256,2048]{1,0:T(8,128)}) %all-reduce.3.cloned.1.call-update) | async-done | bytes 2097168 | tf_op jit(solution)/shard_map/psum | solution.py:37
  478.0 2.2 multiply_reduce_fusion
  480.2 187.4 %all-reduce = f32[2048]{0:T(1024)S(1)} all-reduce(f32[2048]{0:T(1024)S(1)} %get-tuple-element.3), channel_id=3, replica_groups=mesh['dp'=64,'pipe'=4] {'dp'}, use_global_device_ids=true, to_apply=%region_4.0.clone | all-reduce | flops 2048 | bytes 16384
  667.6 0.6 dynamic-slice_multiply_fusion
  668.2 3.1 divide_convert_fusion
  671.3 219.4 %reduce-scatter.2.cloned.1.call-done = f32[32,2048]{1,0:T(8,128)} async-done(((f32[2048,2048]{1,0:T(8,128)}), f32[32,2048]{1,0:T(8,128)}) %reduce-scatter.2.cloned.1.call-update) | async-done | bytes 262160 | tf_op jit(solution)/shard_map/reduce_scatter | solution.py:42
  890.7 1.7 multiply_bitcast_fusion
  (2 shorter events, 0.0 us)
Async XLA Ops:
  7.2 363.9 %copy-start = (bf16[1,256,2048]{2,1,0:T(8,128)(2,1)S(1)}, bf16[1,256,2048]{2,1,0:T(8,128)(2,1)}, u32[]{:S(2)}) copy-start(bf16[1,256,2048]{2,1,0:T(8,128)(2,1)} %param.7) | copy-start | bytes 3145732
  7.2 363.9 %all-gather.3.cloned.1.call-start = ((), (), s32[]{:S(2)}) async-start(), calls=%async_computation.3 | async-start | bytes 8519680 | tf_op jit(solution)/shard_map/all_gather | solution.py:33
  7.9 470.0 %all-reduce.3.cloned.1.call-start = ((), (), s32[]{:S(2)}) async-start(), calls=%async_computation.1 | async-start | bytes 4194304 | tf_op jit(solution)/shard_map/psum | solution.py:37
  378.2 1.2 copy-start.1
  378.2 1.5 copy-start.2
  378.2 512.4 %reduce-scatter.2.cloned.1.call-start = ((), (), s32[]{:S(2)}) async-start(), calls=%async_computation.2 | async-start | bytes 17039360 | tf_op jit(solution)/shard_map/reduce_scatter | solution.py:42
  388.1 0.7 copy-start.3
Sparse Core Ops, SparseCore 0:
  9.8 361.2 all-gather.2
  378.3 99.5 all-reduce.2
  480.5 410.0 reduce-scatter.1
where the time goes:
time: 899 us
  waiting for transfers between devices  671 us (75%)
  blocking collectives  187 us (21%)
  matrix products  15.5 us (2%)
  between operations  14.4 us (2%)
    all_gather x1, waiting for transfers between devices, local(): lax.all_gather(projection, 'dp', axis=0, tiled=True)  363 us
    reduce_scatter x1, waiting for transfers between devices, local(): lax.psum_scatter(weight_term(encoded, cotangent), 'dp', scatter_dimension...  219 us
    unnamed x1, blocking collectives  187 us
    psum x1, waiting for transfers between devices, local(): grad_encoded = lax.psum(partial_value, 'pipe')  87.9 us
  transfers between devices with their start and end apart: 3, of which 3 were waited for; matrix products, arithmetic and copies ran while one was open for 2% of the time, Pallas kernels for 0%

commit v1 on v0

--- a/solution.py
+++ b/solution.py
@@ -4,6 +4,18 @@
 from jax.sharding import PartitionSpec as P
 
 epsilon = 1e-06
+
+
+def assign_trails(mesh_name, raw, row_dim):
+    return jnp.concatenate(
+        lax.all_to_all(
+            jnp.stack(tuple((raw for _ in range(lax.axis_size(mesh_name)))), 0),
+            axis_name=mesh_name,
+            split_axis=0,
+            concat_axis=0,
+        ),
+        axis=row_dim,
+    )
 
 
 def norm_backward(grad_rows, normed_rows, scale_rows, gain):
@@ -30,7 +42,7 @@
     average = 1.0 / lax.axis_size("dp")
     partial_value = lax.dot_general(
         cotangent,
-        lax.all_gather(projection, "dp", axis=0, tiled=True),
+        assign_trails("dp", projection, 0),
         (((1,), (1,)), ((), ())),
         preferred_element_type=jnp.float32,
     )

time: 899 us -> 679 us (0.76)
  waiting for transfers between devices: 671 us -> 249 us
  blocking collectives: 187 us -> 383 us
    all_gather x1 -> x0, waiting for transfers between devices: 363 us -> none  [local(): lax.all_gather(projection, 'dp', axis=0, tiled=True)]
    all_to_all x0 -> x1, blocking collectives: none -> 197 us  [assign_trails(): lax.all_to_all(jnp.stack(tuple((raw for _ in range(lax.axis_size(mesh_nam...]
    reduce_scatter x1, waiting for transfers between devices: 219 us -> 161 us  [local(): lax.psum_scatter(weight_term(encoded, cotangent), 'dp', scatter_dimension...]
  transfers between devices with their start and end apart: 3 -> 2, of which waited for: 3 -> 2; matrix products, arithmetic and copies ran while one was open for 2% -> 2% of each run, Pallas kernels for 0% -> 0%
where the time goes in v1:
time: 679 us; the launch traced here: 673 us
  blocking collectives  383 us (56%)
  waiting for transfers between devices  249 us (37%)
  between operations  16.2 us (2%)
  matrix products  12.1 us (2%)
  other arithmetic  7.9 us (1%)
    all_to_all x1, blocking collectives, assign_trails(): lax.all_to_all(jnp.stack(tuple((raw for _ in range(lax.axis_size(mesh_nam...  197 us
    unnamed x1, blocking collectives  186 us
    reduce_scatter x1, waiting for transfers between devices, local(): lax.psum_scatter(weight_term(encoded, cotangent), 'dp', scatter_dimension...  161 us
    psum x1, waiting for transfers between devices, local(): grad_encoded = lax.psum(partial_value, 'pipe')  88.5 us
  transfers between devices with their start and end apart: 2, of which 2 were waited for; matrix products, arithmetic and copies ran while one was open for 2% of the time, Pallas kernels for 0%

profile of v1, /device:TPU:0, one launch (start us, length us, event | category | flops | bytes accessed | tf_op | source)
XLA Modules:
  0.0 673.3 jit_solution(12812859549229055097)
XLA Ops:
  8.0 0.0 copy-start
  8.0 0.0 all-reduce.3.cloned.1.call-start
  8.1 2.0 stack.3
  10.1 197.0 %all_to_all.5 = bf16[64,32,2048]{2,1,0:T(8,128)(2,1)S(1)} all-to-all(bf16[64,32,2048]{2,1,0:T(8,128)(2,1)S(1)} %stack.3), channel_id=1, replica_groups=mesh['dp'=64,'pipe'=4] {'dp'}, dimensions={0} | all-to-all | bytes 16777216 | tf_op jit(solution)/shard_map/all_to_all | solution.py:11
  207.0 0.0 copy-done
  207.1 3.7 fusion.3
  210.7 0.0 copy-start.1
  210.7 0.0 copy-start.2
  210.7 0.0 all-reduce.3.cloned.1.call-update
  210.7 0.0 reduce-scatter.2.cloned.1.call-start
  210.8 1.1 copy-done.1
  211.9 0.3 fusion
  212.2 0.0 copy-done.2
  212.2 8.4 %fusion.1 = f32[2048,2048]{1,0:T(8,128)} fusion(bf16[1,256,2048]{2,1,0:T(8,128)(2,1)S(1)} %copy-done, f32[2048]{0:T(1024)S(1)} %copy-done.2, bf16[256,2048]{1,0:T(8,128)(2,1)S(1)} %copy-done.1, f32[256]{0:T(256)S(1)} %add_sqrt_fusion), kind=kOutput, calls=%fused_computation.7 | convolution fusion | flops 2149580800 | bytes 18883584 | tf_op jit(solution)/shard_map/dot_general | solution.py:30
  220.7 0.0 copy-start.3
  220.7 0.0 reduce-scatter.2.cloned.1.call-update
  220.7 0.6 copy-done.3
  221.3 0.6 dynamic-slice
  222.6 88.5 %all-reduce.3.cloned.1.call-done = f32[256,2048]{1,0:T(8,128)} async-done(((f32[256,2048]{1,0:T(8,128)}), f32[256,2048]{1,0:T(8,128)}) %all-reduce.3.cloned.1.call-update) | async-done | bytes 2097168 | tf_op jit(solution)/shard_map/psum | solution.py:49
  311.1 2.3 multiply_reduce_fusion
  313.3 186.4 %all-reduce = f32[2048]{0:T(1024)S(1)} all-reduce(f32[2048]{0:T(1024)S(1)} %get-tuple-element.3), channel_id=2, replica_groups=mesh['dp'=64,'pipe'=4] {'dp'}, use_global_device_ids=true, to_apply=%region_4.0.clone | all-reduce | flops 2048 | bytes 16384
  499.7 0.6 dynamic-slice_multiply_fusion
  500.3 3.1 divide_convert_fusion
  503.4 160.8 %reduce-scatter.2.cloned.1.call-done = f32[32,2048]{1,0:T(8,128)} async-done(((f32[2048,2048]{1,0:T(8,128)}), f32[32,2048]{1,0:T(8,128)}) %reduce-scatter.2.cloned.1.call-update) | async-done | bytes 262160 | tf_op jit(solution)/shard_map/reduce_scatter | solution.py:54
  664.2 1.7 multiply_bitcast_fusion
  (2 shorter events, 0.0 us)
Async XLA Ops:
  8.0 199.1 %copy-start = (bf16[1,256,2048]{2,1,0:T(8,128)(2,1)S(1)}, bf16[1,256,2048]{2,1,0:T(8,128)(2,1)}, u32[]{:S(2)}) copy-start(bf16[1,256,2048]{2,1,0:T(8,128)(2,1)} %param.7) | copy-start | bytes 3145732
  8.0 303.0 %all-reduce.3.cloned.1.call-start = ((), (), s32[]{:S(2)}) async-start(), calls=%async_computation.2 | async-start | bytes 4194304 | tf_op jit(solution)/shard_map/psum | solution.py:49
  210.7 1.2 copy-start.1
  210.7 1.5 copy-start.2
  210.7 453.5 %reduce-scatter.2.cloned.1.call-start = ((), (), s32[]{:S(2)}) async-start(), calls=%async_computation.3 | async-start | bytes 17039360 | tf_op jit(solution)/shard_map/reduce_scatter | solution.py:54
  220.7 0.7 copy-start.3
Sparse Core Ops, SparseCore 0:
  210.9 100.1 all-reduce.2
Sparse Core Ops, SparseCore 1:
  220.8 443.4 reduce-scatter.1
